TPU v7x, 128 devices: a whole 4x4x4 slice. The times are simulated.
128 devices in a mesh: req: 16 (over x_hi, y, core), tensor: 8 (over x_lo, z).
Axes of the slice: x: 4 (x_hi: 2, x_lo: 2; x = x_hi * 2 + x_lo), y: 4, z: 4, core: 2. Of those that a mesh axis runs over, the one named last changes fastest.
Arguments:
- hidden: bfloat16 [32, 512, 1792], P('req', 'tensor')
- suffix_len: int32 [32], P('req'), may hold values from 1 to 512, as said below
- request_group: int32 [32], P('req'), may hold values from 0 to 63
- group_slot: int32 [64], replicated, may hold values from 0 to 63, each once
- norm_first: float32 [1792], replicated, may hold values from 0.5 to 2
- query_weight: bfloat16 [1792, 256], P(None, 'tensor'), may hold values from -0.125 to 0.125
- key_weight: bfloat16 [1792, 256], P(None, 'tensor'), may hold values from -0.125 to 0.125
- value_weight: bfloat16 [1792, 1792], P(None, 'tensor'), may hold values from -0.125 to 0.125
- filter_gate: bfloat16 [1792, 1792], P(None, 'tensor'), may hold values from -0.125 to 0.125
- filter_taps: float32 [3, 1792], P(None, 'tensor'), may hold values from -3 to 3
- linear_out: bfloat16 [1792, 1792], P('tensor'), may hold values from -0.125 to 0.125
- norm_second: float32 [1792], replicated, may hold values from 0.5 to 1.5
- window_query: bfloat16 [1792, 1792], P(None, 'tensor')
- window_key: bfloat16 [1792, 1792], P(None, 'tensor')
- window_value: bfloat16 [1792, 1792], P(None, 'tensor'), may hold values from -0.125 to 0.125
- window_out: bfloat16 [1792, 1792], P('tensor'), may hold values from -0.125 to 0.125
- norm_third: float32 [1792], replicated, may hold values from 0.5 to 1.5
- gate_weight: bfloat16 [1792, 7168], P(None, 'tensor'), may hold values from -0.125 to 0.125
- up_weight: bfloat16 [1792, 7168], P(None, 'tensor'), may hold values from -0.125 to 0.125
- down_weight: bfloat16 [7168, 1792], P('tensor'), may hold values from -0.0625 to 0.0625
- prefix_sums: float32 [64, 16, 273, 112], P('req', 'tensor'), as said below
- prefix_norms: float32 [64, 16, 273], P('req', 'tensor'), as said below
- prefix_keys: bfloat16 [64, 64, 1792], P('req', None, 'tensor'), may hold values from -6 to 6
- prefix_values: bfloat16 [64, 64, 1792], P('req', None, 'tensor'), may hold values from -6 to 6
- prefix_tail: bfloat16 [64, 2, 1792], P('req', None, 'tensor'), may hold values from -10 to 10
Outputs:
- hidden_out: bfloat16 [32, 512, 1792], P('req', 'tensor')
- final_norm: float32 [32], P('req')
- top_logit: float32 [32], P('req')
Inputs may be any that keep to these rules, and one draw needn't show every extreme that they name: `suffix_len`: each request's suffix is either a short one of at most 32 tokens or a long one of more than 384; some request has exactly 512. `group_slot`: each slot holds exactly one group. `prefix_sums`: A sum over 128 prefix tokens of the key feature map times the value. `prefix_norms`: A sum over the same 128 tokens of the key feature map, so its inner product with any feature map is positive.
All inputs are finite; a program needn't handle non-finite values.
Results may differ from a plain program's by a relative error of at most 0.024.
Values may be sent and summed in bfloat16 or wider, within the bound.
A program may use at most 128 MiB of HBM per device.

v0:
```python
import jax
import jax.numpy as jnp
from jax import lax
from jax.sharding import PartitionSpec as P

D = 1792
FD = 16
HS = 112
WIN = 64
KC = 3
LMAX = 512
EPS = 1e-05


def rms_norm(row_block, gain_vector):
    floats = row_block.astype(jnp.float32)
    inverse_rms = lax.rsqrt(jnp.mean(floats * floats, axis=-1, keepdims=True) + EPS)
    return (floats * inverse_rms * gain_vector).astype(jnp.bfloat16)


def features(vectors):
    floats = vectors.astype(jnp.float32)
    dimension = floats.shape[-1]
    constant = jnp.ones(floats.shape[:-1] + (1,), jnp.float32)
    linear_part = floats * dimension ** (-0.25)
    square_part = (floats[..., :, None] * floats[..., None, :]).reshape(
        floats.shape[:-1] + (dimension * dimension,)
    )
    square_part = square_part * (2.0 * dimension) ** (-0.5)
    return jnp.concatenate([constant, linear_part, square_part], axis=-1)


def slot_lookup(groups, group_slot):
    matches = jnp.arange(group_slot.shape[0])[None, :] == groups[:, None]
    return jnp.sum(jnp.where(matches, group_slot[None, :], 0), axis=1)


def per_device(
    hidden,
    suffix_len,
    request_group,
    group_slot,
    norm_first,
    query_weight,
    key_weight,
    value_weight,
    filter_gate,
    filter_taps,
    linear_out,
    norm_second,
    window_query,
    window_key,
    window_value,
    window_out,
    norm_third,
    gate_weight,
    up_weight,
    down_weight,
    prefix_sums,
    prefix_norms,
    prefix_keys,
    prefix_values,
    prefix_tail,
):
    requests_here = hidden.shape[0]
    share_rows = hidden.shape[1]
    model_width = hidden.shape[2]
    lin_heads = prefix_sums.shape[1]
    win_heads = prefix_keys.shape[2] // HS
    slot_ids = slot_lookup(request_group, group_slot)
    all_sums, all_norms = (
        lax.all_gather(prefix_sums.astype(jnp.bfloat16), "req", axis=0, tiled=True).astype(
            prefix_sums.dtype
        ),
        lax.all_gather(prefix_norms.astype(jnp.bfloat16), "req", axis=0, tiled=True).astype(
            prefix_norms.dtype
        ),
    )
    all_keys, all_values, all_tails = (
        lax.all_gather(prefix_keys, "req", axis=0, tiled=True),
        lax.all_gather(prefix_values, "req", axis=0, tiled=True),
        lax.all_gather(prefix_tail, "req", axis=0, tiled=True),
    )
    picked_sum = jnp.take(all_sums, slot_ids, axis=0)
    picked_norm = jnp.take(all_norms, slot_ids, axis=0)
    picked_keys = jnp.take(all_keys, slot_ids, axis=0)
    picked_values = jnp.take(all_values, slot_ids, axis=0)
    picked_tail = jnp.take(all_tails, slot_ids, axis=0)

    def settle(stream, partial_sum, gain_vector):
        summed = lax.psum(partial_sum.astype(jnp.bfloat16), "tensor").astype(jnp.float32)
        stream = (stream.astype(jnp.float32) + summed).astype(jnp.bfloat16)
        normed = None if gain_vector is None else rms_norm(stream, gain_vector)
        return (stream, normed)

    stream = lax.all_gather(hidden, "tensor", axis=1, tiled=True)
    normed = rms_norm(stream, norm_first)
    position = jnp.arange(LMAX)
    causal = position[:, None] >= position[None, :]
    key_place = jnp.arange(WIN + LMAX)
    allowed = (key_place[None, :] > position[:, None]) & (
        key_place[None, :] <= position[:, None] + WIN
    )

    def project(normed_rows, matrix):
        flat_rows = normed_rows.reshape(requests_here * LMAX, model_width)
        return jnp.dot(flat_rows, matrix, preferred_element_type=jnp.float32).astype(jnp.bfloat16)

    queries = project(normed, query_weight).reshape(requests_here, LMAX, lin_heads, FD)
    key_rows = project(normed, key_weight).reshape(requests_here, LMAX, lin_heads, FD)
    values_lin = project(normed, value_weight).reshape(requests_here, LMAX, lin_heads * HS)
    gating = project(normed, filter_gate).reshape(requests_here, LMAX, lin_heads * HS)
    extended = jnp.concatenate([picked_tail, values_lin], axis=1).astype(jnp.float32)
    convolved = sum(
        (
            filter_taps[offset] * extended[:, KC - 1 - offset : KC - 1 - offset + LMAX]
            for offset in range(KC)
        )
    )
    mixed_values = (
        (convolved * jax.nn.silu(gating.astype(jnp.float32)))
        .astype(jnp.bfloat16)
        .reshape(requests_here, LMAX, lin_heads, HS)
    )
    scores = jnp.einsum(
        "rthf,rshf->rhts", queries, key_rows, preferred_element_type=jnp.float32
    ) * FD ** (-0.5)
    weights_lin = jnp.where(causal, 1.0 + scores + 0.5 * scores * scores, 0.0)
    numerator = jnp.einsum(
        "rhts,rshd->rthd",
        weights_lin.astype(jnp.bfloat16),
        mixed_values,
        preferred_element_type=jnp.float32,
    )
    denominator = jnp.transpose(jnp.sum(weights_lin, axis=-1), (0, 2, 1))
    mapped = features(queries)
    numerator = numerator + jnp.einsum(
        "rthf,rhfd->rthd", mapped, picked_sum, precision=lax.Precision.HIGHEST
    )
    denominator = denominator + jnp.einsum(
        "rthf,rhf->rth", mapped, picked_norm, precision=lax.Precision.HIGHEST
    )
    linear_rows = (
        (numerator / denominator[..., None])
        .astype(jnp.bfloat16)
        .reshape(requests_here * LMAX, lin_heads * HS)
    )
    partial_sum = jnp.dot(linear_rows, linear_out, preferred_element_type=jnp.float32).reshape(
        requests_here, LMAX, model_width
    )
    stream, normed = settle(stream, partial_sum, norm_second)
    window_q = project(normed, window_query).reshape(requests_here, LMAX, win_heads, HS)
    window_k = project(normed, window_key).reshape(requests_here, LMAX, win_heads * HS)
    window_v = project(normed, window_value).reshape(requests_here, LMAX, win_heads * HS)
    all_keys = jnp.concatenate([picked_keys, window_k], axis=1).reshape(
        requests_here, WIN + LMAX, win_heads, HS
    )
    all_values = jnp.concatenate([picked_values, window_v], axis=1).reshape(
        requests_here, WIN + LMAX, win_heads, HS
    )
    logits = jnp.einsum(
        "rthd,rphd->rhtp", window_q, all_keys, preferred_element_type=jnp.float32
    ) * HS ** (-0.5)
    logits = jnp.where(allowed, logits, -jnp.inf)
    row_max = jnp.max(logits, axis=-1, keepdims=True)
    exponent = jnp.exp(logits - row_max)
    probabilities = (exponent / jnp.sum(exponent, axis=-1, keepdims=True)).astype(jnp.bfloat16)
    attended = jnp.einsum(
        "rhtp,rphd->rthd", probabilities, all_values, preferred_element_type=jnp.float32
    ).astype(jnp.bfloat16)
    attended = attended.reshape(requests_here * LMAX, win_heads * HS)
    final_whole = position[None, :] == suffix_len[:, None] - 1
    local_top = jnp.max(jnp.where(final_whole[:, None, :], row_max[..., 0], -jnp.inf), axis=(1, 2))
    partial_sum = jnp.dot(attended, window_out, preferred_element_type=jnp.float32).reshape(
        requests_here, LMAX, model_width
    )
    stream, normed = settle(stream, partial_sum, norm_third)
    flat_rows = normed.reshape(requests_here * LMAX, model_width)
    gate_rows = jnp.dot(flat_rows, gate_weight, preferred_element_type=jnp.float32)
    up_rows = jnp.dot(flat_rows, up_weight, preferred_element_type=jnp.float32)
    inner_rows = (jax.nn.silu(gate_rows) * up_rows).astype(jnp.bfloat16)
    partial_sum = jnp.dot(inner_rows, down_weight, preferred_element_type=jnp.float32).reshape(
        requests_here, LMAX, model_width
    )
    stream, unused = settle(stream, partial_sum, None)
    row_start = lax.axis_index("tensor") * share_rows
    stream = lax.dynamic_slice_in_dim(stream, row_start, share_rows, 1)
    rows_here = row_start + jnp.arange(share_rows)
    valid = rows_here[None, :] < suffix_len[:, None]
    hidden_out = jnp.where(valid[..., None], stream, jnp.zeros_like(stream))
    stream_f = stream.astype(jnp.float32)
    live_term = jnp.sum(jnp.where(valid[..., None], stream_f * stream_f, 0.0), axis=(1, 2))
    squares = lax.psum(live_term, "tensor")
    top_logit = lax.pmax(local_top, "tensor")
    return (hidden_out, jnp.sqrt(squares / D), top_logit)


def solution(mesh):
    return jax.shard_map(
        per_device,
        mesh=mesh,
        in_specs=(
            P("req", "tensor", None),
            P("req"),
            P("req"),
            P(),
            P(),
            P(None, "tensor"),
            P(None, "tensor"),
            P(None, "tensor"),
            P(None, "tensor"),
            P(None, "tensor"),
            P("tensor", None),
            P(),
            P(None, "tensor"),
            P(None, "tensor"),
            P(None, "tensor"),
            P("tensor", None),
            P(),
            P(None, "tensor"),
            P(None, "tensor"),
            P("tensor", None),
            P("req", "tensor", None, None),
            P("req", "tensor", None),
            P("req", None, "tensor"),
            P("req", None, "tensor"),
            P("req", None, "tensor"),
        ),
        out_specs=(P("req", "tensor", None), P("req"), P("req")),
        check_vma=False,
    )
```

profile of v0, /device:TPU:0, one launch (start us, length us, event | category | flops | bytes accessed | tf_op | source)
XLA Modules:
  0.0 618.0 jit_solution(13063100441761800405)
XLA Ops:
  14.8 25.2 %all_gather.21 = bf16[64,2,273]{2,1,0:T(2,128)(2,1)S(1)} all-gather(bf16[4,2,273]{2,1,0:T(2,128)(2,1)S(1)} %convert_element_type.142), channel_id=1, replica_groups=mesh['req'=16,'tensor'=8] {'req'}, dimensions={0}, use_global_device_ids=true | all-gather | bytes 74256 | tf_op jit(solution)/shard_map/all_gather | solution.py:75
  40.1 20.3 %all_gather.19 = bf16[64,2,224]{2,1,0:T(2,128)(2,1)S(1)} all-gather(bf16[4,2,224]{2,1,0:T(2,128)(2,1)} %param.51), channel_id=1, replica_groups=mesh['req'=16,'tensor'=8] {'req'}, dimensions={0}, use_global_device_ids=true | all-gather | bytes 60928 | tf_op jit(solution)/shard_map/all_gather | solution.py:82
  62.6 3.0 fusion
  69.6 3.9 convolution_convert_fusion.8
  75.0 3.5 convolution_convert_fusion.7
  88.3 48.6 %all-gather.7.cloned.1.call-done = bf16[64,2,273,112]{3,1,2,0:T(2,128)(2,1)} async-done(((bf16[4,2,273,112]{3,1,2,0:T(2,128)(2,1)}), bf16[64,2,273,112]{3,1,2,0:T(2,128)(2,1)}) %all-gather.7.cloned.1.call-update) | async-done | bytes 7827472 | tf_op jit(solution)/shard_map/all_gather | solution.py:72
  137.0 9.5 %convert_element_type.140 = f32[64,2,273,112]{3,1,2,0:T(2,128)} convert(bf16[64,2,273,112]{3,1,2,0:T(2,128)(2,1)} %all-gather.7.cloned.1.call-done) | non-fusion elementwise | flops 3913728 | bytes 23482368 | tf_op jit(solution)/shard_map/convert_element_type | solution.py:72
  146.5 8.2 %gather_fusion.1 = f32[2,2,273,112]{3,1,2,0:T(2,128)} fusion(f32[64,2,273,112]{3,1,2,0:T(2,128)} %convert_element_type.140, s32[1024]{0:T(1024)} %copy-done.19), kind=kCustom, calls=%fused_computation.3 | custom fusion | bytes 978440 | tf_op jit(solution)/shard_map/jit(_take)/gather | solution.py:84
  156.1 4.0 fusion.23
  160.2 3.0 convolution_convert_fusion.2
  163.5 21.2 %all-gather.9.cloned.1.call-done = bf16[64,64,224]{2,1,0:T(8,128)(2,1)} async-done(((bf16[4,64,224]{2,1,0:T(8,128)(2,1)}), bf16[64,64,224]{2,1,0:T(8,128)(2,1)}) %all-gather.9.cloned.1.call-update) | async-done | bytes 1835024 | tf_op jit(solution)/shard_map/all_gather | solution.py:81
  187.5 45.8 %all-gather.11.cloned.1.call-done = bf16[64,64,224]{2,1,0:T(8,128)(2,1)} async-done(((bf16[4,64,224]{2,1,0:T(8,128)(2,1)}), bf16[64,64,224]{2,1,0:T(8,128)(2,1)}) %all-gather.11.cloned.1.call-update) | async-done | bytes 1835024 | tf_op jit(solution)/shard_map/all_gather | solution.py:80
  240.8 90.9 %all-reduce.4.cloned.1.call-done = bf16[2,512,1792]{2,1,0:T(8,128)(2,1)} async-done(((bf16[2,512,1792]{2,1,0:T(8,128)(2,1)}), bf16[2,512,1792]{2,1,0:T(8,128)(2,1)}) %all-reduce.4.cloned.1.call-update) | async-done | bytes 3670032 | tf_op jit(solution)/shard_map/psum | solution.py:91
  331.7 4.5 fusion.4
  345.9 4.3 convolution_convert_fusion.4
  352.3 4.3 convolution_convert_fusion.5
  365.0 3.0 convolution_convert_fusion.1
  368.3 96.2 %all-reduce.6.cloned.1.call-done = bf16[2,512,1792]{2,1,0:T(8,128)(2,1)} async-done(((bf16[2,512,1792]{2,1,0:T(8,128)(2,1)}), bf16[2,512,1792]{2,1,0:T(8,128)(2,1)}) %all-reduce.6.cloned.1.call-update) | async-done | bytes 3670032 | tf_op jit(solution)/shard_map/psum | solution.py:91
  464.5 7.4 %fusion.9 = (f32[2,512,1792]{2,1,0:T(8,128)}, f32[2,512]{1,0:T(2,128)S(1)}) fusion(bf16[2,512,1792]{2,1,0:T(8,128)(2,1)} %all-reduce.6.cloned.1.call-done, bf16[2,512,1792]{2,1,0:T(8,128)(2,1)} %copy-done.3), kind=kLoop, calls=%fused_computation.29 | loop fusion | flops 12844032 | bytes 14684160 | tf_op jit(solution)/shard_map/convert_element_type | solution.py:92
  475.1 5.9 fusion.68
  481.0 12.5 %convolution_convert_fusion = bf16[1024,1792]{1,0:T(8,128)(2,1)} fusion(bf16[896,1792]{1,0:T(8,128)(2,1)S(1)} %copy-done, f32[1024,896]{1,0:T(8,128)} %fusion.68, bf16[1024,1792]{1,0:T(8,128)(2,1)} %bitcast.103, bf16[1792,896]{1,0:T(8,128)(2,1)} %param.45), kind=kOutput, calls=%fused_computation.26 | convolution fusion | flops 6584008704 | bytes 17432576 | tf_op jit(solution)/shard_map/dot_general | solution.py:182
  494.4 18.8 %pmax.7 = f32[2]{0:T(128)} all-reduce(f32[2]{0:T(128)S(1)} %select_reduce_fusion.1), channel_id=1, replica_groups=mesh['req'=16,'tensor'=8] {'tensor'}, use_global_device_ids=true, to_apply=%region_13.15 | all-reduce | flops 2 | bytes 16 | tf_op jit(solution)/shard_map/pmax | solution.py:194
  513.1 77.0 %all-reduce.8.cloned.1.call-done = bf16[2,512,1792]{2,1,0:T(8,128)(2,1)} async-done(((bf16[2,512,1792]{2,1,0:T(8,128)(2,1)}), bf16[2,512,1792]{2,1,0:T(8,128)(2,1)}) %all-reduce.8.cloned.1.call-update) | async-done | bytes 3670032 | tf_op jit(solution)/shard_map/psum | solution.py:91
  592.7 17.9 %psum.31 = f32[2]{0:T(128)S(1)} all-reduce(f32[2]{0:T(128)S(1)} %get-tuple-element.4), channel_id=1, replica_groups=mesh['req'=16,'tensor'=8] {'tensor'}, use_global_device_ids=true, to_apply=%region_11.13 | all-reduce | flops 2 | bytes 16 | tf_op jit(solution)/shard_map/psum | solution.py:193
  (137 shorter events, 64.4 us)
Async XLA Ops:
  7.2 473.8 %copy-start = (bf16[896,1792]{1,0:T(8,128)(2,1)S(1)}, bf16[896,1792]{1,0:T(8,128)(2,1)}, u32[]{:S(2)}) copy-start(bf16[896,1792]{1,0:T(8,128)(2,1)} %param.46) | copy-start | bytes 9633796
  7.2 54.8 %copy-start.23 = (f32[3,224]{1,0:T(4,128)S(1)}, f32[3,224]{1,0:T(4,128)}, u32[]{:S(2)}) copy-start(f32[3,224]{1,0:T(4,128)} %param.36) | copy-start | bytes 8068
  7.2 58.4 %copy-start.16 = (f32[1792]{0:T(1024)S(1)}, f32[1792]{0:T(1024)}, u32[]{:S(2)}) copy-start(f32[1792]{0:T(1024)} %param.31) | copy-start | bytes 21508
  7.2 55.4 %all-gather.5.cloned.1.call-start = ((), (), s32[]{:S(2)}) async-start(), calls=%async_computation | async-start | bytes 4128768 | tf_op jit(solution)/shard_map/all_gather | solution.py:96
  7.9 129.0 %all-gather.7.cloned.1.call-start = ((), (), s32[]{:S(2)}) async-start(), calls=%async_computation.1 | async-start | bytes 9504768 | tf_op jit(solution)/shard_map/all_gather | solution.py:72
  10.6 174.1 %all-gather.9.cloned.1.call-start = ((), (), s32[]{:S(2)}) async-start(), calls=%async_computation.3 | async-start | bytes 2228224 | tf_op jit(solution)/shard_map/all_gather | solution.py:81
  11.4 222.0 %all-gather.11.cloned.1.call-start = ((), (), s32[]{:S(2)}) async-start(), calls=%async_computation.4 | async-start | bytes 2228224 | tf_op jit(solution)/shard_map/all_gather | solution.py:80
  11.9 319.8 %all-reduce.4.cloned.1.call-start = ((), (), s32[]{:S(2)}) async-start(), calls=%async_computation.2 | async-start | bytes 7340032 | tf_op jit(solution)/shard_map/psum | solution.py:91
  14.1 46.9 %copy-start.19 = (s32[1024]{0:T(1024)}, s32[1024]{0:T(1024)S(1)}, u32[]{:S(2)}) copy-start(s32[1024]{0:T(1024)S(1)} %pad_clamp_fusion.1) | copy-start | bytes 12292
  62.6 3.1 copy-start.5
  65.7 2.7 copy-start.14
  78.5 3.5 copy-start.12
  78.5 3.4 copy-start.15
  82.0 2.3 copy-start.25
  154.7 5.5 copy-start.10
  160.2 3.1 copy-start.29
  163.3 301.3 %all-reduce.6.cloned.1.call-start = ((), (), s32[]{:S(2)}) async-start(), calls=%async_computation.5 | async-start | bytes 7340032 | tf_op jit(solution)/shard_map/psum | solution.py:91
  240.8 95.4 %copy-start.17 = (f32[1792]{0:T(1024)S(1)}, f32[1792]{0:T(1024)}, u32[]{:S(2)}) copy-start(f32[1792]{0:T(1024)} %param.38) | copy-start | bytes 21508
  336.3 3.7 copy-start.26
  368.0 103.9 %copy-start.18 = (f32[1792]{0:T(1024)S(1)}, f32[1792]{0:T(1024)}, u32[]{:S(2)}) copy-start(f32[1792]{0:T(1024)} %param.43) | copy-start | bytes 21508
  368.0 222.1 %all-reduce.8.cloned.1.call-start = ((), (), s32[]{:S(2)}) async-start(), calls=%async_computation.6 | async-start | bytes 7340032 | tf_op jit(solution)/shard_map/psum | solution.py:91
  464.5 7.4 %copy-start.4 = (bf16[2,512,1792]{2,1,0:T(8,128)(2,1)S(1)}, bf16[2,512,1792]{2,1,0:T(8,128)(2,1)}, u32[]{:S(2)}) copy-start(bf16[2,512,1792]{2,1,0:T(8,128)(2,1)} %copy-done.3) | copy-start | bytes 11010052
  464.5 7.4 %copy-start.6 = (bf16[2,512,1792]{2,1,0:T(8,128)(2,1)S(1)}, bf16[2,512,1792]{2,1,0:T(8,128)(2,1)}, u32[]{:S(2)}) copy-start(bf16[2,512,1792]{2,1,0:T(8,128)(2,1)} %all-reduce.6.cloned.1.call-done) | copy-start | bytes 11010052
  472.0 3.2 copy-start.24
  (13 other events, 20.7 us)
Sparse Core Ops, SparseCore 0:
  9.7 50.9 all-gather.4
  63.0 73.8 all-gather.6
  139.4 45.2 all-gather.8
  187.0 46.2 all-gather.10
  235.7 95.9 all-reduce.3
  368.1 96.3 all-reduce.5
  493.6 96.4 all-reduce.7
where the time goes:
time: 619 us; the launch traced here: 618 us
  waiting for transfers between devices  382 us (62%)
  blocking collectives  82.2 us (13%)
  matrix products  57.9 us (9%)
  other arithmetic  41.5 us (7%)
  local copies, waits for them, and re-layouts  39.4 us (6%)
  between operations  14.6 us (2%)
    psum x3, waiting for transfers between devices, settle(): lax.psum(partial_sum.astype(jnp.bfloat16), 'tensor').astype(jnp.float32)  264 us
    all_gather x1, waiting for transfers between devices, per_device(): lax.all_gather(prefix_sums.astype(jnp.bfloat16), 'req', axis=0, tiled=True)  48.6 us
    all_gather x1, waiting for transfers between devices, per_device(): lax.all_gather(prefix_keys, 'req', axis=0, tiled=True)  45.8 us
    all_gather x1, blocking collectives, per_device(): lax.all_gather(prefix_norms.astype(jnp.bfloat16), 'req', axis=0, tiled=True)  25.2 us
    all_gather x1, waiting for transfers between devices, per_device(): lax.all_gather(prefix_values, 'req', axis=0, tiled=True)  21.2 us
    all_gather x1, blocking collectives, per_device(): lax.all_gather(prefix_tail, 'req', axis=0, tiled=True)  20.3 us
    dot_general x7, matrix products, project(): jnp.dot(flat_rows, matrix, preferred_element_type=jnp.float32)  20.3 us
    pmax x1, blocking collectives, per_device(): top_logit = lax.pmax(local_top, 'tensor')  18.8 us
  transfers between devices with their start and end apart: 7, of which 6 were waited for; matrix products, arithmetic and copies ran while one was open for 11% of the time, Pallas kernels for 0%

commit v1 on v0

--- a/solution.py
+++ b/solution.py
@@ -10,6 +10,11 @@
 KC = 3
 LMAX = 512
 EPS = 1e-05
+
+
+def gather_and_add(x, mesh_axis):
+    parts = lax.all_gather(x, mesh_axis)
+    return jnp.sum(parts, axis=0)
 
 
 def rms_norm(row_block, gain_vector):
@@ -88,7 +93,7 @@
     picked_tail = jnp.take(all_tails, slot_ids, axis=0)
 
     def settle(stream, partial_sum, gain_vector):
-        summed = lax.psum(partial_sum.astype(jnp.bfloat16), "tensor").astype(jnp.float32)
+        summed = gather_and_add(partial_sum.astype(jnp.bfloat16), "tensor").astype(jnp.float32)
         stream = (stream.astype(jnp.float32) + summed).astype(jnp.bfloat16)
         normed = None if gain_vector is None else rms_norm(stream, gain_vector)
         return (stream, normed)

time: 619 us -> 1240 us (2.00)
  waiting for transfers between devices: 382 us -> 945 us
  other arithmetic: 41.5 us -> 94.2 us
    all_gather x0 -> x3, waiting for transfers between devices: none -> 838 us  [gather_and_add(): parts = lax.all_gather(x, mesh_axis)]
    psum x3 -> x0, waiting for transfers between devices: 264 us -> none  [settle(): lax.psum(partial_sum.astype(jnp.bfloat16), 'tensor').astype(jnp.float32)]
    reduce_sum x0 -> x3, other arithmetic: none -> 38.8 us  [gather_and_add(): return jnp.sum(parts, axis=0)]
    all_gather x1, waiting for transfers between devices: 45.8 us -> 9.35 us  [per_device(): lax.all_gather(prefix_keys, 'req', axis=0, tiled=True)]
    all_gather x1, waiting for transfers between devices: 21.2 us -> 45.8 us  [per_device(): lax.all_gather(prefix_values, 'req', axis=0, tiled=True)]
  transfers between devices with their start and end apart: 7 -> 7, of which waited for: 6 -> 6; matrix products, arithmetic and copies ran while one was open for 11% -> 6% of each run, Pallas kernels for 0% -> 0%
where the time goes in v1:
time: 1240 us; the launch traced here: 1230 us
  waiting for transfers between devices  945 us (76%)
  other arithmetic  94.2 us (8%)
  blocking collectives  79.9 us (6%)
  matrix products  55 us (4%)
  local copies, waits for them, and re-layouts  39.6 us (3%)
  between operations  15 us (1%)
    all_gather x3, waiting for transfers between devices, gather_and_add(): parts = lax.all_gather(x, mesh_axis)  838 us
    all_gather x1, waiting for transfers between devices, per_device(): lax.all_gather(prefix_sums.astype(jnp.bfloat16), 'req', axis=0, tiled=True)  49.6 us
    all_gather x1, waiting for transfers between devices, per_device(): lax.all_gather(prefix_values, 'req', axis=0, tiled=True)  45.8 us
    reduce_sum x3, other arithmetic, gather_and_add(): return jnp.sum(parts, axis=0)  38.8 us
    all_gather x1, blocking collectives, per_device(): lax.all_gather(prefix_tail, 'req', axis=0, tiled=True)  25.2 us
  transfers between devices with their start and end apart: 7, of which 6 were waited for; matrix products, arithmetic and copies ran while one was open for 6% of the time, Pallas kernels for 0%

profile of v1, /device:TPU:0, one launch (start us, length us, event | category | flops | bytes accessed | tf_op | source)
XLA Modules:
  0.0 1228.7 jit_solution(9914443987479524082)
XLA Ops:
  15.7 25.2 %all_gather.35 = bf16[64,2,224]{2,1,0:T(2,128)(2,1)S(1)} all-gather(bf16[4,2,224]{2,1,0:T(2,128)(2,1)} %param.51), channel_id=1, replica_groups=mesh['req'=16,'tensor'=8] {'req'}, dimensions={0}, use_global_device_ids=true | all-gather | bytes 60928 | tf_op jit(solution)/shard_map/all_gather | solution.py:87
  40.9 20.4 %all_gather.37 = bf16[64,2,273]{2,1,0:T(2,128)(2,1)S(1)} all-gather(bf16[4,2,273]{2,1,0:T(2,128)(2,1)S(1)} %convert_element_type.155), channel_id=1, replica_groups=mesh['req'=16,'tensor'=8] {'req'}, dimensions={0}, use_global_device_ids=true | all-gather | bytes 74256 | tf_op jit(solution)/shard_map/all_gather | solution.py:80
  63.0 3.0 fusion
  70.7 3.5 convolution_convert_fusion.9
  74.2 3.5 convolution_convert_fusion.7
  87.5 49.6 %all-gather.12.cloned.1.call-done = bf16[64,2,273,112]{3,1,2,0:T(2,128)(2,1)} async-done(((bf16[4,2,273,112]{3,1,2,0:T(2,128)(2,1)}), bf16[64,2,273,112]{3,1,2,0:T(2,128)(2,1)}) %all-gather.12.cloned.1.call-update) | async-done | bytes 7827472 | tf_op jit(solution)/shard_map/all_gather | solution.py:77
  137.1 21.5 %convert_element_type.153 = f32[64,2,273,112]{3,1,2,0:T(2,128)} convert(bf16[64,2,273,112]{3,1,2,0:T(2,128)(2,1)} %all-gather.12.cloned.1.call-done) | non-fusion elementwise | flops 3913728 | bytes 23482368 | tf_op jit(solution)/shard_map/convert_element_type | solution.py:77
  158.6 8.0 gather_fusion.1
  168.1 4.0 fusion.23
  175.5 9.4 all-gather.16.cloned.1.call-done
  187.6 45.8 %all-gather.14.cloned.1.call-done = bf16[64,64,224]{2,1,0:T(8,128)(2,1)} async-done(((bf16[4,64,224]{2,1,0:T(8,128)(2,1)}), bf16[64,64,224]{2,1,0:T(8,128)(2,1)}) %all-gather.14.cloned.1.call-update) | async-done | bytes 1835024 | tf_op jit(solution)/shard_map/all_gather | solution.py:86
  241.0 281.5 %all-gather.20.cloned.1.call-done = bf16[16,512,1792]{2,1,0:T(8,128)(2,1)} async-done(((bf16[2,512,1792]{2,1,0:T(8,128)(2,1)}), bf16[16,512,1792]{2,1,0:T(8,128)(2,1)}) %all-gather.20.cloned.1.call-update) | async-done | bytes 29360144 | tf_op jit(solution)/shard_map/all_gather | solution.py:16
  522.5 12.8 %reduce_sum.105 = bf16[2,512,1792]{2,1,0:T(8,128)(2,1)} reduce(bf16[8,2,512,1792]{3,2,1,0:T(8,128)(2,1)} %bitcast.98, bf16[]{:T(256)} %constant.94.clone.1), dimensions={0}, to_apply=%region_3.4 | reduce | flops 12845056 | bytes 33030146 | tf_op jit(solution)/shard_map/reduce_sum | solution.py:17
  535.3 4.5 fusion.4
  549.6 4.2 convolution_convert_fusion.4
  570.2 287.4 %all-gather.22.cloned.1.call-done = bf16[16,512,1792]{2,1,0:T(8,128)(2,1)} async-done(((bf16[2,512,1792]{2,1,0:T(8,128)(2,1)}), bf16[16,512,1792]{2,1,0:T(8,128)(2,1)}) %all-gather.22.cloned.1.call-update) | async-done | bytes 29360144 | tf_op jit(solution)/shard_map/all_gather | solution.py:16
  857.6 13.1 %reduce_sum.108 = bf16[2,512,1792]{2,1,0:T(8,128)(2,1)} reduce(bf16[8,2,512,1792]{3,2,1,0:T(8,128)(2,1)} %bitcast.99, bf16[]{:T(256)} %constant.94.clone.1), dimensions={0}, to_apply=%region_7.9 | reduce | flops 12845056 | bytes 33030146 | tf_op jit(solution)/shard_map/reduce_sum | solution.py:17
  870.7 7.4 fusion.9
  881.4 5.8 fusion.68
  887.1 12.5 %convolution_convert_fusion = bf16[1024,1792]{1,0:T(8,128)(2,1)} fusion(bf16[896,1792]{1,0:T(8,128)(2,1)S(1)} %copy-done, f32[1024,896]{1,0:T(8,128)} %fusion.68, bf16[1024,1792]{1,0:T(8,128)(2,1)} %bitcast.107, bf16[1792,896]{1,0:T(8,128)(2,1)} %param.45), kind=kOutput, calls=%fused_computation.26 | convolution fusion | flops 6584008704 | bytes 17432576 | tf_op jit(solution)/shard_map/dot_general | solution.py:187
  900.5 17.6 %pmax.7 = f32[2]{0:T(128)} all-reduce(f32[2]{0:T(128)S(1)} %select_reduce_fusion.1), channel_id=1, replica_groups=mesh['req'=16,'tensor'=8] {'tensor'}, use_global_device_ids=true, to_apply=%region_13.15 | all-reduce | flops 2 | bytes 16 | tf_op jit(solution)/shard_map/pmax | solution.py:199
  918.2 269.2 %all-gather.18.cloned.1.call-done = bf16[8,2,512,1792]{3,2,1,0:T(8,128)(2,1)} async-done(((bf16[1,2,512,1792]{3,2,1,0:T(8,128)(2,1)}), bf16[8,2,512,1792]{3,2,1,0:T(8,128)(2,1)}) %all-gather.18.cloned.1.call-update) | async-done | bytes 29360144 | tf_op jit(solution)/shard_map/all_gather | solution.py:16
  1187.3 12.9 %reduce_sum.110 = bf16[2,512,1792]{2,1,0:T(8,128)(2,1)} reduce(bf16[8,2,512,1792]{3,2,1,0:T(8,128)(2,1)} %all-gather.18.cloned.1.call-done, bf16[]{:T(256)} %constant.94.clone.1), dimensions={0}, to_apply=%region_9.11 | reduce | flops 12845056 | bytes 33030146 | tf_op jit(solution)/shard_map/reduce_sum | solution.py:17
  1202.5 16.6 %psum.7 = f32[2]{0:T(128)S(1)} all-reduce(f32[2]{0:T(128)S(1)} %get-tuple-element.4), channel_id=1, replica_groups=mesh['req'=16,'tensor'=8] {'tensor'}, use_global_device_ids=true, to_apply=%region_11.13 | all-reduce | flops 2 | bytes 16 | tf_op jit(solution)/shard_map/psum | solution.py:198
  (140 shorter events, 74.2 us)
Async XLA Ops:
  7.2 880.0 %copy-start = (bf16[896,1792]{1,0:T(8,128)(2,1)S(1)}, bf16[896,1792]{1,0:T(8,128)(2,1)}, u32[]{:S(2)}) copy-start(bf16[896,1792]{1,0:T(8,128)(2,1)} %param.46) | copy-start | bytes 9633796
  7.2 58.8 %copy-start.18 = (f32[1792]{0:T(1024)S(1)}, f32[1792]{0:T(1024)}, u32[]{:S(2)}) copy-start(f32[1792]{0:T(1024)} %param.31) | copy-start | bytes 21508
  7.2 55.8 %all-gather.10.cloned.1.call-start = ((), (), s32[]{:S(2)}) async-start(), calls=%async_computation | async-start | bytes 4128768 | tf_op jit(solution)/shard_map/all_gather | solution.py:101
  7.9 129.1 %all-gather.12.cloned.1.call-start = ((), (), s32[]{:S(2)}) async-start(), calls=%async_computation.1 | async-start | bytes 9504768 | tf_op jit(solution)/shard_map/all_gather | solution.py:77
  10.6 174.2 %all-gather.16.cloned.1.call-start = ((), (), s32[]{:S(2)}) async-start(), calls=%async_computation.3 | async-start | bytes 2228224 | tf_op jit(solution)/shard_map/all_gather | solution.py:85
  11.4 222.0 %all-gather.14.cloned.1.call-start = ((), (), s32[]{:S(2)}) async-start(), calls=%async_computation.2 | async-start | bytes 2228224 | tf_op jit(solution)/shard_map/all_gather | solution.py:86
  12.0 510.5 %all-gather.20.cloned.1.call-start = ((), (), s32[]{:S(2)}) async-start(), calls=%async_computation.5 | async-start | bytes 33030144 | tf_op jit(solution)/shard_map/all_gather | solution.py:16
  12.9 2.9 copy-start.28
  63.0 3.1 copy-start.6
  66.1 2.7 copy-start.16
  77.7 3.5 copy-start.14
  77.7 3.4 copy-start.17
  166.6 5.6 copy-start.11
  172.2 3.1 copy-start.29
  175.2 682.4 %all-gather.22.cloned.1.call-start = ((), (), s32[]{:S(2)}) async-start(), calls=%async_computation.6 | async-start | bytes 33030144 | tf_op jit(solution)/shard_map/all_gather | solution.py:16
  535.3 4.6 copy-start.19
  539.9 3.6 copy-start.25
  547.6 6.2 copy-start.9
  547.6 6.2 copy-start.26
  570.1 617.2 %all-gather.18.cloned.1.call-start = ((), (), s32[]{:S(2)}) async-start(), calls=%async_computation.4 | async-start | bytes 33030144 | tf_op jit(solution)/shard_map/all_gather | solution.py:16
  870.7 7.4 copy-start.4
  870.7 7.5 copy-start.5
  870.7 7.5 copy-start.20
  878.2 3.2 copy-start.23
  (13 other events, 21.4 us)
Sparse Core Ops, SparseCore 0:
  9.6 50.9 all-gather.9
  63.0 73.9 all-gather.11
  139.5 45.2 all-gather.15
  187.1 46.2 all-gather.13
  234.9 287.4 all-gather.19
  570.3 287.3 all-gather.21
  899.8 287.5 all-gather.17
